TPU v7x, 32 devices: a whole 2x2x4 slice. The times are simulated.
32 devices in a mesh: wide: 8 (over z, x), grp: 4 (over y, core).
Axes of the slice: x: 2, y: 2, z: 4, core: 2. Of those that a mesh axis runs over, the one named last changes fastest.
Arguments:
- query_rows: bfloat16 [4096, 1280], P(('wide', 'grp')), may hold values from -9 to 9, as said below
- key_rows: bfloat16 [4096, 1280], P(('wide', 'grp')), may hold values from -9 to 9, as said below
- value_rows: bfloat16 [4096, 1280], P(('wide', 'grp')), may hold values from -6 to 6
- block_image: int32 [32], replicated, may hold values from 0 to 6, never falling along the last dimension, each value on 1 to 8 neighbouring positions
Outputs:
- attended: bfloat16 [4096, 1280], P(('wide', 'grp'))
Inputs may be any that keep to these rules, and one draw needn't show every extreme that they name: `query_rows`: Queries: entries bounded as stated. `key_rows`: Keys: entries bounded as stated. `block_image`: image numbers never fall along the window; every image covers 1 to 8 whole blocks and one covers exactly 8.
All inputs are finite; a program needn't handle non-finite values.
Results may differ from a plain program's by a relative error of at most 0.004.
Values may be sent and summed in bfloat16 or wider, within the bound.
A program may use at most 64 MiB of HBM per device.

v0:
```python
import math

import jax
import jax.numpy as jnp
from jax import lax
from jax.sharding import PartitionSpec as P

HDIM = 80
BLK = 128
MOST = 8


neg_large = -1e30


def from_behind(value, axis, steps):
    count = lax.axis_size(axis)
    leading, last = (max(0, -steps), min(count, count - steps))
    return lax.ppermute(value, axis, [(source, source + steps) for source in range(leading, last)])


def block_tokens(block_ids, block_rows):
    return jnp.broadcast_to(block_ids[:, None], (block_ids.shape[0], block_rows)).reshape(-1)


def fold_tile(totals, query_ids, query_head, key_head, value_head, key_ids, scale_value):
    live_pairs = query_ids[:, None] == key_ids[None, :]
    acc_out, run_max, run_den = totals
    scores = (
        jnp.einsum("qhd,khd->qhk", query_head, key_head, preferred_element_type=jnp.float32)
        * scale_value
    )
    scores = jnp.where(live_pairs[:, None, :], scores, neg_large)
    new_max = jnp.maximum(run_max, jnp.max(scores, axis=-1))
    weights = jnp.where(live_pairs[:, None, :], jnp.exp(scores - new_max[..., None]), 0.0)
    fading = jnp.exp(run_max - new_max)
    run_den = run_den * fading + jnp.sum(weights, axis=-1)
    acc_out = acc_out * fading[..., None] + jnp.einsum(
        "qhk,khd->qhd", weights.astype(jnp.bfloat16), value_head, preferred_element_type=jnp.float32
    )
    return (acc_out, new_max, run_den)


def fold_keys(totals, query_ids, query_head, key_head, value_head, key_ids, scale_value):
    current = tuple((member for member in totals))
    current = fold_tile(current, query_ids, query_head, key_head, value_head, key_ids, scale_value)
    return current


def body(query_rows, key_rows, value_rows, block_image):
    stacked = jnp.stack((query_rows, key_rows, value_rows))
    regrouped = lax.all_to_all(stacked, "grp", split_axis=2, concat_axis=1, tiled=True)
    local_rows = regrouped.shape[1]
    head_count = regrouped.shape[2] // HDIM
    shaped = regrouped.reshape(3, local_rows, head_count, HDIM)
    query_head = shaped[0]
    key_value = shaped[1:]
    blocks_here = local_rows // BLK
    wide_count = lax.axis_size("wide")
    position = lax.axis_index("wide")
    scale_value = 1.0 / math.sqrt(HDIM)
    query_ids = block_tokens(
        lax.dynamic_slice_in_dim(block_image, position * blocks_here, blocks_here), BLK
    )

    def source_ids(source):
        inside = (source >= 0) & (source < wide_count)
        clipped = jnp.clip(source, 0, wide_count - 1)
        found_ids = block_tokens(
            lax.dynamic_slice_in_dim(block_image, clipped * blocks_here, blocks_here), BLK
        )
        return jnp.where(inside, found_ids, -2)

    totals = (
        jnp.zeros((local_rows, head_count, HDIM), jnp.float32),
        jnp.full((local_rows, head_count), neg_large, jnp.float32),
        jnp.zeros((local_rows, head_count), jnp.float32),
    )
    reach_steps = min(wide_count - 1, (MOST + blocks_here - 2) // blocks_here)
    totals = fold_keys(
        totals, query_ids, query_head, key_value[0], key_value[1], query_ids, scale_value
    )
    for distance in range(1, reach_steps + 1):
        arrived = from_behind(key_value, "wide", distance)
        totals = fold_keys(
            totals,
            query_ids,
            query_head,
            arrived[0],
            arrived[1],
            source_ids(position - distance),
            scale_value,
        )
        arrived = from_behind(key_value, "wide", -distance)
        totals = fold_keys(
            totals,
            query_ids,
            query_head,
            arrived[0],
            arrived[1],
            source_ids(position + distance),
            scale_value,
        )
    acc_out, run_max, run_den = totals
    result = (
        (acc_out / run_den[..., None]).astype(jnp.bfloat16).reshape(local_rows, head_count * HDIM)
    )
    restored = lax.all_to_all(result, "grp", split_axis=0, concat_axis=1, tiled=True)
    return restored


def solution(mesh):
    return jax.shard_map(
        body,
        mesh=mesh,
        in_specs=(
            P(("wide", "grp"), None),
            P(("wide", "grp"), None),
            P(("wide", "grp"), None),
            P(),
        ),
        out_specs=P(("wide", "grp"), None),
        check_vma=False,
    )
```

profile of v0, /device:TPU:24, one launch (start us, length us, event | category | flops | bytes accessed | tf_op | source)
XLA Modules:
  0.0 93.7 jit_solution(12908256977121639371)
XLA Ops:
  0.0 0.0 copy-start
  0.0 1.3 %pad_maximum_fusion = bf16[3,128,1280]{2,1,0:T(8,128)(2,1)S(1)} fusion(bf16[1,128,1280]{2,1,0:T(8,128)(2,1)} %bitcast.190, bf16[1,128,1280]{2,1,0:T(8,128)(2,1)} %bitcast.191, bf16[1,128,1280]{2,1,0:T(8,128)(2,1)} %bitcast.192), kind=kLoop, calls=%fused_computation.51 | loop fusion | flops 983040 | bytes 1966080 | tf_op jit(solution)/shard_map/stack | solution.py:51
  1.3 2.2 %copy.41 = bf16[3,128,1280]{1,0,2:T(4,128)(2,1)} copy(bf16[3,128,1280]{2,1,0:T(8,128)(2,1)S(1)} %pad_maximum_fusion) | data formatting | bytes 1966080 | tf_op jit(solution)/shard_map/stack | solution.py:51
  3.5 3.5 %all-to-all-start = ((bf16[3,128,1280]{1,0,2:T(4,128)(2,1)}), bf16[3,128,1280]{1,0,2:T(4,128)(2,1)S(1)}, u32[]{:S(2)}, u32[]{:S(2)}) async-start(bf16[3,128,1280]{1,0,2:T(4,128)(2,1)} %copy.41), calls=%async_computation | async-start | bytes 2621440 | tf_op jit(solution)/shard_map/all_to_all | solution.py:52
  7.0 0.0 copy-done
  7.1 0.1 broadcast_select_fusion.3
  7.1 0.1 broadcast_bitcast_fusion.4
  7.2 0.1 broadcast_bitcast_fusion.2
  7.3 0.1 broadcast_bitcast_fusion
  7.4 16.9 %all-to-all-done = bf16[3,128,1280]{1,0,2:T(4,128)(2,1)S(1)} async-done(((bf16[3,128,1280]{1,0,2:T(4,128)(2,1)}), bf16[3,128,1280]{1,0,2:T(4,128)(2,1)S(1)}, u32[]{:S(2)}, u32[]{:S(2)}) %all-to-all-start) | async-done | bytes 983072 | tf_op jit(solution)/shard_map/all_to_all | solution.py:52
  24.2 0.1 copy.42
  24.4 0.5 copy.47
  24.9 1.1 %slice.48 = bf16[2,512,4,80]{1,3,2,0:T(8,128)(2,1)} reshape(bf16[2,4,128,320]{2,1,3,0:T(4,128)(2,1)S(1)} %copy.47) | data formatting | bytes 1310720 | tf_op jit(solution)/shard_map/slice | solution.py:57
  26.0 3.3 %collective-permute-start.1 = (bf16[2,512,4,80]{1,3,2,0:T(8,128)(2,1)}, bf16[2,512,4,80]{1,3,2,0:T(8,128)(2,1)}, u32[]{:S(2)}, u32[]{:S(2)}) collective-permute-start(bf16[2,512,4,80]{1,3,2,0:T(8,128)(2,1)} %slice.48), channel_id=1, source_target_pairs={{4,0},{8,4},{12,8},{16,12},{20,16},{24,20},{28,24},{5,1},{9,5},{13... | collective-permute-start | bytes 1966088 | tf_op jit(solution)/shard_map/ppermute | solution.py:19
  29.3 0.9 broadcast_compare_fusion.4
  30.2 3.2 %collective-permute-start.3 = (bf16[2,512,4,80]{1,3,2,0:T(8,128)(2,1)}, bf16[2,512,4,80]{1,3,2,0:T(8,128)(2,1)}, u32[]{:S(2)}, u32[]{:S(2)}) collective-permute-start(bf16[2,512,4,80]{1,3,2,0:T(8,128)(2,1)} %slice.48), channel_id=1, source_target_pairs={{8,0},{12,4},{16,8},{20,12},{24,16},{28,20},{9,1},{13,5},{17,9},{2... | collective-permute-start | bytes 1966088 | tf_op jit(solution)/shard_map/ppermute | solution.py:19
  33.4 1.3 %collective-permute-start.2 = (bf16[2,512,4,80]{1,3,2,0:T(8,128)(2,1)}, bf16[2,512,4,80]{1,3,2,0:T(8,128)(2,1)}, u32[]{:S(2)}, u32[]{:S(2)}) collective-permute-start(bf16[2,512,4,80]{1,3,2,0:T(8,128)(2,1)} %slice.48), channel_id=1, source_target_pairs={{0,8},{4,12},{8,16},{12,20},{16,24},{20,28},{1,9},{5,13},{9,17},{1... | collective-permute-start | bytes 1966088 | tf_op jit(solution)/shard_map/ppermute | solution.py:19
  34.7 2.7 %collective-permute-start = (bf16[2,512,4,80]{1,3,2,0:T(8,128)(2,1)}, bf16[2,512,4,80]{1,3,2,0:T(8,128)(2,1)}, u32[]{:S(2)}, u32[]{:S(2)}) collective-permute-start(bf16[2,512,4,80]{1,3,2,0:T(8,128)(2,1)} %slice.48), channel_id=1, source_target_pairs={{0,4},{4,8},{8,12},{12,16},{16,20},{20,24},{24,28},{1,5},{5,9},{9,... | collective-permute-start | bytes 1966088 | tf_op jit(solution)/shard_map/ppermute | solution.py:19
  37.5 0.1 fusion.100
  37.5 0.3 copy.45
  37.8 0.1 squeeze.35
  37.9 0.3 copy.44
  38.2 0.1 squeeze.34
  38.3 0.3 copy.43
  38.6 0.1 squeeze.33
  38.7 1.0 %fusion = (f32[512,4]{0,1:T(4,128)S(1)}, f32[4,512,512]{2,1,0:T(8,128)S(1)}) fusion(pred[512,512]{0,1:T(8,128)(4,1)S(1)} %get-tuple-element.19, bf16[512,4,80]{0,2,1:T(8,128)(2,1)S(1)} %squeeze.33, bf16[512,4,80]{0,2,1:T(8,128)(2,1)S(1)} %squeeze.34), kind=kOutput, calls=%fused_computation.10 | convolution fusion | flops 170915840 | bytes 5120000 | tf_op jit(solution)/shard_map/qhd,khd->qhk/dot_general | solution.py:30
  39.7 5.1 %collective-permute-done.1 = bf16[2,512,4,80]{1,3,2,0:T(8,128)(2,1)} collective-permute-done((bf16[2,512,4,80]{1,3,2,0:T(8,128)(2,1)}, bf16[2,512,4,80]{1,3,2,0:T(8,128)(2,1)}, u32[]{:S(2)}, u32[]{:S(2)}) %collective-permute-start.1) | collective-permute-done | bytes 655392 | tf_op jit(solution)/shard_map/ppermute | solution.py:19
  44.8 1.9 %fusion.2 = (f32[512,4]{0,1:T(4,128)S(1)}, f32[4,512,512]{2,1,0:T(8,128)S(1)}) fusion(pred[512,512]{0,1:T(8,128)(4,1)S(1)} %get-tuple-element.20, bf16[512,4,80]{0,2,1:T(8,128)(2,1)S(1)} %squeeze.34, bf16[2,512,4,80]{1,3,2,0:T(8,128)(2,1)} %collective-permute-done.1), kind=kOutput, calls=%fused_computation.12 | convolution fusion | flops 170915840 | bytes 5120000 | tf_op jit(solution)/shard_map/qhd,khd->qhk/dot_general | solution.py:30
  46.7 4.5 %collective-permute-done.2 = bf16[2,512,4,80]{1,3,2,0:T(8,128)(2,1)} collective-permute-done((bf16[2,512,4,80]{1,3,2,0:T(8,128)(2,1)}, bf16[2,512,4,80]{1,3,2,0:T(8,128)(2,1)}, u32[]{:S(2)}, u32[]{:S(2)}) %collective-permute-start.2) | collective-permute-done | bytes 655392 | tf_op jit(solution)/shard_map/ppermute | solution.py:19
  51.2 1.9 %fusion.3 = (f32[512,4]{0,1:T(4,128)S(1)}, f32[4,512,512]{2,1,0:T(8,128)S(1)}) fusion(pred[512,512]{0,1:T(8,128)(4,1)S(1)} %get-tuple-element.21, bf16[512,4,80]{0,2,1:T(8,128)(2,1)S(1)} %squeeze.34, bf16[2,512,4,80]{1,3,2,0:T(8,128)(2,1)} %collective-permute-done.2), kind=kOutput, calls=%fused_computation.13 | convolution fusion | flops 170915840 | bytes 5120000 | tf_op jit(solution)/shard_map/qhd,khd->qhk/dot_general | solution.py:30
  53.2 4.2 %collective-permute-done.3 = bf16[2,512,4,80]{1,3,2,0:T(8,128)(2,1)} collective-permute-done((bf16[2,512,4,80]{1,3,2,0:T(8,128)(2,1)}, bf16[2,512,4,80]{1,3,2,0:T(8,128)(2,1)}, u32[]{:S(2)}, u32[]{:S(2)}) %collective-permute-start.3) | collective-permute-done | bytes 655392 | tf_op jit(solution)/shard_map/ppermute | solution.py:19
  57.4 1.9 %fusion.4 = (f32[512,4]{0,1:T(4,128)S(1)}, f32[4,512,512]{2,1,0:T(8,128)S(1)}) fusion(pred[512,512]{0,1:T(8,128)(4,1)S(1)} %get-tuple-element.22, bf16[512,4,80]{0,2,1:T(8,128)(2,1)S(1)} %squeeze.34, bf16[2,512,4,80]{1,3,2,0:T(8,128)(2,1)} %collective-permute-done.3), kind=kOutput, calls=%fused_computation.14 | convolution fusion | flops 170915840 | bytes 5120000 | tf_op jit(solution)/shard_map/qhd,khd->qhk/dot_general | solution.py:30
  59.4 6.0 %collective-permute-done = bf16[2,512,4,80]{1,3,2,0:T(8,128)(2,1)} collective-permute-done((bf16[2,512,4,80]{1,3,2,0:T(8,128)(2,1)}, bf16[2,512,4,80]{1,3,2,0:T(8,128)(2,1)}, u32[]{:S(2)}, u32[]{:S(2)}) %collective-permute-start) | collective-permute-done | bytes 655392 | tf_op jit(solution)/shard_map/ppermute | solution.py:19
  65.4 1.9 %fusion.1 = (f32[512,4]{0,1:T(4,128)S(1)}, f32[4,512,512]{2,1,0:T(8,128)S(1)}) fusion(pred[512,512]{0,1:T(8,128)(4,1)S(1)} %get-tuple-element.23, bf16[512,4,80]{0,2,1:T(8,128)(2,1)S(1)} %squeeze.34, bf16[2,512,4,80]{1,3,2,0:T(8,128)(2,1)} %collective-permute-done), kind=kOutput, calls=%fused_computation.11 | convolution fusion | flops 170915840 | bytes 5120000 | tf_op jit(solution)/shard_map/qhd,khd->qhk/dot_general | solution.py:30
  67.4 1.0 %fusion.13 = f32[512,4]{0,1:T(4,128)S(1)} fusion(f32[4,512,512]{2,1,0:T(8,128)S(1)} %get-tuple-element.30, f32[512,4]{0,1:T(4,128)S(1)} %get-tuple-element.10, pred[512,512]{0,1:T(8,128)(4,1)S(1)} %get-tuple-element.22), kind=kLoop, calls=%fused_computation.23 | loop fusion | flops 5240832 | bytes 4472832 | tf_op jit(solution)/shard_map/reduce_sum | solution.py:37
  68.4 1.1 %fusion.11 = f32[512,4]{0,1:T(4,128)S(1)} fusion(f32[4,512,512]{2,1,0:T(8,128)S(1)} %get-tuple-element.32, f32[512,4]{0,1:T(4,128)S(1)} %get-tuple-element.11, pred[512,512]{0,1:T(8,128)(4,1)S(1)} %get-tuple-element.21), kind=kLoop, calls=%fused_computation.21 | loop fusion | flops 5240832 | bytes 4472832 | tf_op jit(solution)/shard_map/reduce_sum | solution.py:37
  69.5 1.0 %fusion.9 = f32[512,4]{0,1:T(4,128)S(1)} fusion(f32[4,512,512]{2,1,0:T(8,128)S(1)} %get-tuple-element.34, f32[512,4]{0,1:T(4,128)S(1)} %get-tuple-element.12, pred[512,512]{0,1:T(8,128)(4,1)S(1)} %get-tuple-element.20), kind=kLoop, calls=%fused_computation.19 | loop fusion | flops 5240832 | bytes 4472832 | tf_op jit(solution)/shard_map/reduce_sum | solution.py:37
  70.5 1.1 %fusion.5 = f32[512,4]{0,1:T(4,128)S(1)} fusion(f32[4,512,512]{2,1,0:T(8,128)S(1)} %get-tuple-element.38, f32[512,4]{0,1:T(4,128)S(1)} %get-tuple-element.18, pred[512,512]{0,1:T(8,128)(4,1)S(1)} %get-tuple-element.19), kind=kLoop, calls=%fused_computation.15 | loop fusion | flops 5240832 | bytes 4472832 | tf_op jit(solution)/shard_map/reduce_sum | solution.py:37
  71.6 1.1 %fusion.7 = f32[512,4]{0,1:T(4,128)S(1)} fusion(f32[4,512,512]{2,1,0:T(8,128)S(1)} %get-tuple-element.36, f32[512,4]{0,1:T(4,128)S(1)} %get-tuple-element.13, pred[512,512]{0,1:T(8,128)(4,1)S(1)} %get-tuple-element.23), kind=kLoop, calls=%fused_computation.17 | loop fusion | flops 5240832 | bytes 4472832 | tf_op jit(solution)/shard_map/reduce_sum | solution.py:37
  72.7 1.5 %fusion.69 = f32[512,4,80]{0,2,1:T(8,128)S(1)} fusion(bf16[512,4,80]{0,2,1:T(8,128)(2,1)S(1)} %squeeze.35, f32[4,512,512]{2,1,0:T(8,128)S(1)} %get-tuple-element.38, f32[512,4]{0,1:T(4,128)S(1)} %get-tuple-element.18, pred[512,512]{0,1:T(8,128)(4,1)S(1)} %get-tuple-element.19, f32[512,4]{0,1:T(4,128)S(1)} %get-tuple-element.9, ...), kind=kOutput, calls=%fused_computation.48 | convolution fusion | flops 173342720 | bytes 5464064 | tf_op jit(solution)/shard_map/qhk,khd->qhd/dot_general | solution.py:38
  74.2 2.3 %fusion.42 = f32[512,4,80]{0,2,1:T(8,128)S(1)} fusion(f32[4,512,512]{2,1,0:T(8,128)S(1)} %get-tuple-element.30, f32[512,4]{0,1:T(4,128)S(1)} %get-tuple-element.10, pred[512,512]{0,1:T(8,128)(4,1)S(1)} %get-tuple-element.22, bf16[2,512,4,80]{1,3,2,0:T(8,128)(2,1)} %collective-permute-done.3), kind=kOutput, calls=%fused_computation.39 | convolution fusion | flops 173015040 | bytes 5447680 | tf_op jit(solution)/shard_map/qhk,khd->qhd/dot_general | solution.py:38
  76.5 2.3 %fusion.39 = f32[512,4,80]{0,2,1:T(8,128)S(1)} fusion(f32[4,512,512]{2,1,0:T(8,128)S(1)} %get-tuple-element.32, f32[512,4]{0,1:T(4,128)S(1)} %get-tuple-element.11, pred[512,512]{0,1:T(8,128)(4,1)S(1)} %get-tuple-element.21, bf16[2,512,4,80]{1,3,2,0:T(8,128)(2,1)} %collective-permute-done.2), kind=kOutput, calls=%fused_computation.38 | convolution fusion | flops 173015040 | bytes 5447680 | tf_op jit(solution)/shard_map/qhk,khd->qhd/dot_general | solution.py:38
  78.8 2.3 %fusion.36 = f32[512,4,80]{0,2,1:T(8,128)S(1)} fusion(f32[4,512,512]{2,1,0:T(8,128)S(1)} %get-tuple-element.34, f32[512,4]{0,1:T(4,128)S(1)} %get-tuple-element.12, pred[512,512]{0,1:T(8,128)(4,1)S(1)} %get-tuple-element.20, bf16[2,512,4,80]{1,3,2,0:T(8,128)(2,1)} %collective-permute-done.1), kind=kOutput, calls=%fused_computation.37 | convolution fusion | flops 173015040 | bytes 5447680 | tf_op jit(solution)/shard_map/qhk,khd->qhd/dot_general | solution.py:38
  81.1 2.4 %fusion.75 = bf16[512,4,80]{0,2,1:T(8,128)(2,1)S(1)} fusion(f32[512,4,80]{0,2,1:T(8,128)S(1)} %fusion.42, f32[512,4,80]{0,2,1:T(8,128)S(1)} %fusion.39, f32[512,4,80]{0,2,1:T(8,128)S(1)} %fusion.36, f32[512,4,80]{0,2,1:T(8,128)S(1)} %fusion.69, f32[4,512,512]{2,1,0:T(8,128)S(1)} %get-tuple-element.36, f32[512,4]{0,1:T(4,128)S(1)} %get-tuple-element.13, ...), kind=kOutput, calls=%fused_computation.50 | convolution fusion | flops 174489600 | bytes 7774208 | tf_op jit(solution)/shard_map/qhk,khd->qhd/dot_general | solution.py:38
  83.5 0.1 all_to_all.28
  83.7 9.1 %all_to_all.34 = bf16[4,128,320]{1,2,0:T(8,128)(2,1)S(1)} all-to-all(bf16[4,128,320]{1,2,0:T(8,128)(2,1)S(1)} %copy.52), channel_id=1, replica_groups=mesh['wide'=8,'grp'=4] {'grp'}, dimensions={0} | all-to-all | bytes 655360 | tf_op jit(solution)/shard_map/all_to_all | solution.py:108
  92.8 0.9 copy.53
  (4 shorter events, 0.1 us)
Async XLA Ops:
  0.0 7.0 %copy-start = (s32[32]{0:T(128)S(1)}, s32[32]{0:T(128)}, u32[]{:S(2)}) copy-start(s32[32]{0:T(128)} %param.7) | copy-start | bytes 388
  3.5 20.8 %all-to-all-start = ((bf16[3,128,1280]{1,0,2:T(4,128)(2,1)}), bf16[3,128,1280]{1,0,2:T(4,128)(2,1)S(1)}, u32[]{:S(2)}, u32[]{:S(2)}) async-start(bf16[3,128,1280]{1,0,2:T(4,128)(2,1)} %copy.41), calls=%async_computation | async-start | bytes 2621440 | tf_op jit(solution)/shard_map/all_to_all | solution.py:52
  26.0 18.7 %collective-permute-start.1 = (bf16[2,512,4,80]{1,3,2,0:T(8,128)(2,1)}, bf16[2,512,4,80]{1,3,2,0:T(8,128)(2,1)}, u32[]{:S(2)}, u32[]{:S(2)}) collective-permute-start(bf16[2,512,4,80]{1,3,2,0:T(8,128)(2,1)} %slice.48), channel_id=1, source_target_pairs={{4,0},{8,4},{12,8},{16,12},{20,16},{24,20},{28,24},{5,1},{9,5},{13... | collective-permute-start | bytes 1966088 | tf_op jit(solution)/shard_map/ppermute | solution.py:19
  30.2 27.2 %collective-permute-start.3 = (bf16[2,512,4,80]{1,3,2,0:T(8,128)(2,1)}, bf16[2,512,4,80]{1,3,2,0:T(8,128)(2,1)}, u32[]{:S(2)}, u32[]{:S(2)}) collective-permute-start(bf16[2,512,4,80]{1,3,2,0:T(8,128)(2,1)} %slice.48), channel_id=1, source_target_pairs={{8,0},{12,4},{16,8},{20,12},{24,16},{28,20},{9,1},{13,5},{17,9},{2... | collective-permute-start | bytes 1966088 | tf_op jit(solution)/shard_map/ppermute | solution.py:19
  33.4 17.8 %collective-permute-start.2 = (bf16[2,512,4,80]{1,3,2,0:T(8,128)(2,1)}, bf16[2,512,4,80]{1,3,2,0:T(8,128)(2,1)}, u32[]{:S(2)}, u32[]{:S(2)}) collective-permute-start(bf16[2,512,4,80]{1,3,2,0:T(8,128)(2,1)} %slice.48), channel_id=1, source_target_pairs={{0,8},{4,12},{8,16},{12,20},{16,24},{20,28},{1,9},{5,13},{9,17},{1... | collective-permute-start | bytes 1966088 | tf_op jit(solution)/shard_map/ppermute | solution.py:19
  34.7 30.7 %collective-permute-start = (bf16[2,512,4,80]{1,3,2,0:T(8,128)(2,1)}, bf16[2,512,4,80]{1,3,2,0:T(8,128)(2,1)}, u32[]{:S(2)}, u32[]{:S(2)}) collective-permute-start(bf16[2,512,4,80]{1,3,2,0:T(8,128)(2,1)} %slice.48), channel_id=1, source_target_pairs={{0,4},{4,8},{8,12},{12,16},{16,20},{20,24},{24,28},{1,5},{5,9},{9,... | collective-permute-start | bytes 1966088 | tf_op jit(solution)/shard_map/ppermute | solution.py:19
where the time goes:
time: 94.3 us; the launch traced here: 93.7 us
  waiting for transfers between devices  36.7 us (39%)
  matrix products  19.6 us (21%)
  starting transfers between devices  14 us (15%)
  blocking collectives  9.08 us (10%)
  other arithmetic  7.57 us (8%)
  local copies, waits for them, and re-layouts  6.44 us (7%)
    ppermute x4, waiting for transfers between devices, from_behind(): lax.ppermute(value, axis, [(source, source + steps) for source in range(l...  19.9 us
    all_to_all x1, waiting for transfers between devices, body(): lax.all_to_all(stacked, 'grp', split_axis=2, concat_axis=1, tiled=True)  16.9 us
    dot_general x5, matrix products, fold_tile(): jnp.einsum('qhk,khd->qhd', weights.astype(jnp.bfloat16), value_head, pref...  10.9 us
    ppermute x4, starting transfers between devices, from_behind(): lax.ppermute(value, axis, [(source, source + steps) for source in range(l...  10.5 us
    all_to_all x1, blocking collectives, body(): lax.all_to_all(result, 'grp', split_axis=0, concat_axis=1, tiled=True)  9.08 us
    dot_general x5, matrix products, fold_tile(): jnp.einsum('qhd,khd->qhk', query_head, key_head, preferred_element_type=j...  8.72 us
    reduce_sum x5, other arithmetic, fold_tile(): run_den = run_den * fading + jnp.sum(weights, axis=-1)  5.27 us
    all_to_all x1, starting transfers between devices, body(): lax.all_to_all(stacked, 'grp', split_axis=2, concat_axis=1, tiled=True)  3.54 us
  transfers between devices with their start and end apart: 5, of which 5 were waited for; matrix products, arithmetic and copies ran while one was open for 10% of the time, Pallas kernels for 0%

commit v1 on v0

v1 whole, which is shorter than its diff:
```python
import functools
import math

import jax
import jax.numpy as jnp
from jax import lax
from jax.experimental import pallas as pl
from jax.experimental.pallas import tpu as pltpu
from jax.sharding import PartitionSpec as P

HDIM = 80
BLK = 128
MOST = 8
NEG = -1e30
MESH = pl.DeviceIdType.MESH


def kernel(cfg, img, q_in, k_in, v_in, out, kv_src, q_src, kv_own, q_own, halo, kn_own, kn_halo,
           m_scr, l_scr, acc, s_scr, p_scr, o_src, o_own,
           kv_ss, kv_rs, q_ss, q_rs, up_ss, dn_ss, halo_rs, o_ss, o_rs, loc_s):
    planes, fold, grp, heads = cfg
    n = fold * grp
    cols = heads * HDIM
    wide_at, grp_at = lax.axis_index("wide"), lax.axis_index("grp")
    plane = wide_at // fold
    fold_at = wide_at % fold
    me = fold_at * grp + grp_at
    has_prev, has_next = plane > 0, plane < planes - 1

    def device(at_plane, member):
        return (at_plane * fold + member // grp, member % grp)

    offsets = [(a, b) for a in range(fold) for b in range(grp)][1:]

    def to_peer(a, b):
        return ((fold_at + a) % fold) * grp + (grp_at + b) % grp

    def from_peer(a, b):
        return ((fold_at + fold - a) % fold) * grp + (grp_at + grp - b) % grp

    barrier = pltpu.get_barrier_semaphore()
    for a, b in offsets:
        pl.semaphore_signal(barrier, inc=1, device_id=device(plane, to_peer(a, b)), device_id_type=MESH)

    @pl.when(has_prev)
    def _():
        pl.semaphore_signal(barrier, inc=1, device_id=device(plane - 1, me), device_id_type=MESH)

    @pl.when(has_next)
    def _():
        pl.semaphore_signal(barrier, inc=1, device_id=device(plane + 1, me), device_id_type=MESH)

    def turn(ref, store):
        whole = jnp.concatenate([ref[:, c:c + BLK].T for c in range(0, n * cols, BLK)], axis=0)
        for member in range(n):
            store(member, whole[member * cols:(member + 1) * cols])

    def put_k(member, x):
        kv_src[member, 0] = x

    def put_v(member, x):
        kv_src[member, 1] = x

    def put_q(member, x):
        q_src[member] = x

    turn(k_in, put_k)
    turn(v_in, put_v)
    turn(q_in, put_q)

    @pl.when(jnp.logical_not(has_prev))
    def _():
        halo[0:n] = jnp.zeros((n,) + halo.shape[1:], halo.dtype)

    @pl.when(jnp.logical_not(has_next))
    def _():
        halo[n:2 * n] = jnp.zeros((n,) + halo.shape[1:], halo.dtype)

    pl.semaphore_wait(barrier, n - 1 + has_prev.astype(jnp.int32) + has_next.astype(jnp.int32))

    def remote(src, dst, ss, rs, dev):
        return pltpu.make_async_remote_copy(src_ref=src, dst_ref=dst, send_sem=ss, recv_sem=rs,
                                            device_id=dev, device_id_type=MESH)

    def up(member, src):
        return remote(src, halo.at[member], up_ss.at[member], halo_rs.at[member], device(plane + 1, me))

    def down(member, src):
        return remote(src, halo.at[n + member], dn_ss.at[member], halo_rs.at[n + member], device(plane - 1, me))

    def forward(member, src):
        @pl.when(jnp.logical_and(has_next, member >= 1))
        def _():
            up(member, src).start()

        @pl.when(jnp.logical_and(has_prev, member <= n - 2))
        def _():
            down(member, src).start()

    def kv_copy(src, dst):
        return remote(kv_src.at[dst], kv_own.at[src], kv_ss.at[dst], kv_rs.at[src], device(plane, dst))

    def q_copy(src, dst):
        return remote(q_src.at[dst], q_own.at[src], q_ss.at[dst], q_rs.at[src], device(plane, dst))

    forward(me, kv_src.at[me])
    for a, b in offsets:
        kv_copy(me, to_peer(a, b)).start()
    for a, b in offsets:
        q_copy(me, to_peer(a, b)).start()
    keep_kv = pltpu.make_async_copy(kv_src.at[me], kv_own.at[me], loc_s.at[0])
    keep_q = pltpu.make_async_copy(q_src.at[me], q_own.at[me], loc_s.at[1])
    keep_kv.start()
    keep_q.start()
    for a, b in offsets:
        source = from_peer(a, b)
        kv_copy(source, me).wait_recv()
        forward(source, kv_own.at[source])
    keep_kv.wait()
    keep_q.wait()

    def natural(src, dst):
        for h in range(heads):
            dst[h] = src[h * HDIM:(h + 1) * HDIM].T

    @pl.loop(0, n)
    def _(b):
        natural(kv_own.at[b, 0], kn_own.at[b])

    for a, b in offsets:
        q_copy(from_peer(a, b), me).wait_recv()

    factor = math.log2(math.e) / math.sqrt(HDIM)
    blocks = img.shape[0]
    lane = lax.broadcasted_iota(jnp.int32, (1, 2 * BLK), 1)
    base = plane * n

    def live_row(first, key_block):
        inside = jnp.logical_and(key_block >= 0, key_block < blocks)
        key_id = img[jnp.clip(key_block, 0, blocks - 1)]
        key_id = jnp.where(inside, key_id, -2)
        ids = jnp.where(lane < BLK, img[first], img[first + 1])
        return ids == key_id

    def scores_and_max(h, pair, keys, live, start):
        q_pair = jnp.concatenate([q_own[2 * pair, pl.ds(h * HDIM, HDIM)],
                                  q_own[2 * pair + 1, pl.ds(h * HDIM, HDIM)]], axis=1)
        top = start
        for t in range(n):
            s = jnp.dot(keys(t), q_pair, preferred_element_type=jnp.float32)
            s_scr[t] = s
            top = jnp.maximum(top, jnp.where(live[t], jnp.max(s, axis=0, keepdims=True), NEG))
        return top

    def weigh(top, live, values):
        total = jnp.zeros((8, 2 * BLK), jnp.float32)
        for t in range(n):
            shift = jnp.where(live[t], -top * factor, NEG)
            w = jnp.exp2(s_scr[t] * factor + shift)
            total = total + jnp.sum(w.reshape(BLK // 8, 8, 2 * BLK), axis=0)
            p_scr[t * BLK:(t + 1) * BLK] = w.astype(jnp.bfloat16)
        v = jnp.concatenate([values(t) for t in range(n)], axis=1)
        out_t = jnp.dot(v, p_scr[...], preferred_element_type=jnp.float32)
        return out_t, jnp.sum(total, axis=0, keepdims=True)

    def near(step, carry):
        pair = step
        first = base + 2 * pair
        live = [live_row(first, base + t) for t in range(n)]
        for h in range(heads):
            top = scores_and_max(h, pair, lambda t: kn_own[t, h], live, jnp.full((1, 2 * BLK), NEG, jnp.float32))
            out_t, total = weigh(top, live, lambda t: kv_own[t, 1, h * HDIM:(h + 1) * HDIM])
            m_scr[pair * heads + h] = top
            l_scr[pair * heads + h] = total
            acc[pair * heads + h] = out_t
        return carry

    lax.fori_loop(0, n // 2, near, 0)

    for member in range(1, n):
        @pl.when(has_prev)
        def _():
            up(member, kv_own.at[member]).wait_recv()
        natural(halo.at[member, 0], kn_halo.at[member])
    for member in range(n - 1):
        @pl.when(has_next)
        def _():
            down(member, kv_own.at[member]).wait_recv()
        natural(halo.at[n + member, 0], kn_halo.at[n + member])

    def out_copy(src, dst):
        return remote(o_src.at[dst], o_own.at[src], o_ss.at[dst], o_rs.at[src], device(plane, dst))

    def far(step, carry):
        pair = (me // 2 + 1 + step) % (n // 2)
        first = base + 2 * pair
        live = []
        for t in range(n):
            slot = 2 * pair + 1 + t
            live.append(live_row(first, jnp.where(slot < n, base - n + slot, base + slot)))
        for h in range(heads):
            at = pair * heads + h
            top1 = m_scr[at]
            top = scores_and_max(h, pair, lambda t: kn_halo[2 * pair + 1 + t, h], live, top1)
            out_t, total = weigh(top, live, lambda t: halo[2 * pair + 1 + t, 1, h * HDIM:(h + 1) * HDIM])
            fade = jnp.exp2((top1 - top) * factor)
            res = (acc[at] * fade + out_t) / (l_scr[at] * fade + total)
            res = res.astype(jnp.bfloat16)
            o_src[2 * pair, h * HDIM:(h + 1) * HDIM] = res[:, :BLK]
            o_src[2 * pair + 1, h * HDIM:(h + 1) * HDIM] = res[:, BLK:]
        for r in range(2):
            dst = 2 * pair + r

            @pl.when(dst != me)
            def _():
                out_copy(me, dst).start()

            @pl.when(dst == me)
            def _():
                pltpu.make_async_copy(o_src.at[me], o_own.at[me], loc_s.at[2]).start()
        return carry

    lax.fori_loop(0, n // 2, far, 0)

    pltpu.make_async_copy(o_src.at[me], o_own.at[me], loc_s.at[2]).wait()
    for a, b in offsets:
        out_copy(from_peer(a, b), me).wait_recv()
    flat = jnp.concatenate([o_own[member] for member in range(n)], axis=0)
    for c in range(0, n * cols, BLK):
        out[:, c:c + BLK] = flat[c:c + BLK].T

    for a, b in offsets:
        kv_copy(me, to_peer(a, b)).wait_send()
        q_copy(me, to_peer(a, b)).wait_send()
        out_copy(me, to_peer(a, b)).wait_send()

    @pl.when(has_next)
    def _():
        for member in range(1, n):
            up(member, kv_own.at[member]).wait_send()

    @pl.when(has_prev)
    def _():
        for member in range(n - 1):
            down(member, kv_own.at[member]).wait_send()


def solution(mesh):
    wide, grp = mesh.shape["wide"], mesh.shape["grp"]
    fold = MOST // grp
    n = fold * grp
    planes = wide // fold

    def body(query_rows, key_rows, value_rows, block_image):
        rows, width = query_rows.shape
        heads = width // HDIM // n
        cols = heads * HDIM
        bf, f32 = jnp.bfloat16, jnp.float32
        vmem = pl.BlockSpec(memory_space=pltpu.VMEM)
        dma = pltpu.SemaphoreType.DMA
        return pl.pallas_call(
            functools.partial(kernel, (planes, fold, grp, heads)),
            out_shape=jax.ShapeDtypeStruct((rows, width), bf),
            in_specs=[pl.BlockSpec(memory_space=pltpu.SMEM), vmem, vmem, vmem],
            out_specs=vmem,
            scratch_shapes=[
                pltpu.VMEM((n, 2, cols, BLK), bf),
                pltpu.VMEM((n, cols, BLK), bf),
                pltpu.VMEM((n, 2, cols, BLK), bf),
                pltpu.VMEM((n, cols, BLK), bf),
                pltpu.VMEM((2 * n, 2, cols, BLK), bf),
                pltpu.VMEM((n, heads, BLK, HDIM), bf),
                pltpu.VMEM((2 * n, heads, BLK, HDIM), bf),
                pltpu.VMEM((n // 2 * heads, 1, 2 * BLK), f32),
                pltpu.VMEM((n // 2 * heads, 1, 2 * BLK), f32),
                pltpu.VMEM((n // 2 * heads, HDIM, 2 * BLK), f32),
                pltpu.VMEM((n, BLK, 2 * BLK), f32),
                pltpu.VMEM((n * BLK, 2 * BLK), bf),
                pltpu.VMEM((n, cols, BLK), bf),
                pltpu.VMEM((n, cols, BLK), bf),
                dma((n,)), dma((n,)), dma((n,)), dma((n,)),
                dma((n,)), dma((n,)), dma((2 * n,)),
                dma((n,)), dma((n,)), dma((3,)),
            ],
            compiler_params=pltpu.CompilerParams(collective_id=0, has_side_effects=True),
        )(block_image, query_rows, key_rows, value_rows)

    return jax.shard_map(
        body,
        mesh=mesh,
        in_specs=(
            P(("wide", "grp"), None),
            P(("wide", "grp"), None),
            P(("wide", "grp"), None),
            P(),
        ),
        out_specs=P(("wide", "grp"), None),
        check_vma=False,
    )
```

time: 94.3 us -> 34.2 us (0.36)
  the two profiles are of different devices: /device:TPU:24 before, /device:TPU:1 now
where the time goes in v1:
time: 34.2 us; the launch traced here: 34 us
  Pallas kernels  32.3 us (94%)
  local copies, waits for them, and re-layouts  1.72 us (5%)
    pallas_call x1, Pallas kernels, body(): pl.pallas_call(functools.partial(kernel, (planes, fold, grp, heads)), out...  32.3 us
    unnamed x1, local copies, waits for them, and re-layouts  1.72 us

profile of v1, /device:TPU:1, one launch (start us, length us, event | category | flops | bytes accessed | tf_op | source)
XLA Modules:
  0.0 34.0 jit_solution(677880663495687737)
XLA Ops:
  0.0 32.3 %shard_map.46 = bf16[128,1280]{1,0:T(8,128)(2,1)} custom-call(s32[32]{0:T(128)} %img.1, bf16[128,1280]{1,0:T(8,128)(2,1)} %q_in.1, bf16[128,1280]{1,0:T(8,128)(2,1)} %k_in.1, bf16[128,1280]{1,0:T(8,128)(2,1)} %v_in.1), custom_call_target="tpu_custom_call" | custom-call | tf_op jit(solution)/shard_map/pallas_call | solution.py:261
  32.3 1.7 %copy.6 = bf16[128,1280]{1,0:T(8,128)(2,1)} copy(bf16[128,1280]{1,0:T(8,128)(2,1)} %shard_map.46) | data formatting | bytes 655360

commit v2 on v1

v2 whole, which is shorter than its diff:
```python
import functools
import math

import jax
import jax.numpy as jnp
from jax import lax
from jax.experimental import pallas as pl
from jax.experimental.pallas import tpu as pltpu
from jax.sharding import PartitionSpec as P

HDIM = 80
BLK = 128
MOST = 8
NEG = -1e30
MESH = pl.DeviceIdType.MESH


def kernel(cfg, img, q_hbm, k_hbm, v_hbm, out, q_in, k_in, v_in, k_src, q_src, v_src, k_own, q_own, v_own,
           k_halo, v_halo, kn_own, kn_halo, m_scr, l_scr, acc, s_scr, p_near, p_far, o_src, o_own,
           k_ss, k_rs, q_ss, q_rs, v_ss, v_rs, k_up, k_dn, k_hr, v_up, v_dn, v_hr, o_ss, o_rs, loc_s):
    planes, fold, grp, heads = cfg
    n = fold * grp
    cols = heads * HDIM
    wide_at, grp_at = lax.axis_index("wide"), lax.axis_index("grp")
    plane = wide_at // fold
    fold_at = wide_at % fold
    me = fold_at * grp + grp_at
    has_prev, has_next = plane > 0, plane < planes - 1

    loads = [pltpu.make_async_copy(src, dst, loc_s.at[i])
             for i, (src, dst) in enumerate(((k_hbm, k_in), (q_hbm, q_in), (v_hbm, v_in)))]
    for load in loads:
        load.start()

    def device(at_plane, member):
        return (at_plane * fold + member // grp, member % grp)

    def to_peer(i):
        return ((fold_at + i // grp) % fold) * grp + (grp_at + i % grp) % grp

    def from_peer(i):
        return ((fold_at + fold - i // grp) % fold) * grp + (grp_at + grp - i % grp) % grp

    barrier = pltpu.get_barrier_semaphore()
    for i in range(1, n):
        pl.semaphore_signal(barrier, inc=1, device_id=device(plane, to_peer(i)), device_id_type=MESH)

    @pl.when(has_prev)
    def _():
        pl.semaphore_signal(barrier, inc=1, device_id=device(plane - 1, me), device_id_type=MESH)

    @pl.when(has_next)
    def _():
        pl.semaphore_signal(barrier, inc=1, device_id=device(plane + 1, me), device_id_type=MESH)

    def turn(ref, dst):
        whole = jnp.concatenate([ref[:, c:c + BLK].T for c in range(0, n * cols, BLK)], axis=0)
        for member in range(n):
            dst[member] = whole[member * cols:(member + 1) * cols]

    @pl.when(jnp.logical_not(has_prev))
    def _():
        for ref in (k_halo, v_halo):
            ref[0:n] = jnp.zeros((n,) + ref.shape[1:], ref.dtype)

    @pl.when(jnp.logical_not(has_next))
    def _():
        for ref in (k_halo, v_halo):
            ref[n:2 * n] = jnp.zeros((n,) + ref.shape[1:], ref.dtype)

    for load, ref, dst in zip(loads, (k_in, q_in, v_in), (k_src, q_src, v_src)):
        load.wait()
        turn(ref, dst)

    pl.semaphore_wait(barrier, n - 1 + has_prev.astype(jnp.int32) + has_next.astype(jnp.int32))

    def remote(src, dst, ss, rs, dev):
        return pltpu.make_async_remote_copy(src_ref=src, dst_ref=dst, send_sem=ss, recv_sem=rs,
                                            device_id=dev, device_id_type=MESH)

    k_halos, v_halos = (k_halo, k_up, k_dn, k_hr), (v_halo, v_up, v_dn, v_hr)

    def up(halos, member, src):
        halo, ss, _, rs = halos
        return remote(src, halo.at[member], ss.at[member], rs.at[member], device(plane + 1, me))

    def down(halos, member, src):
        halo, _, ss, rs = halos
        return remote(src, halo.at[n + member], ss.at[member], rs.at[n + member], device(plane - 1, me))

    def forward(halos, member, src):
        @pl.when(jnp.logical_and(has_next, member >= 1))
        def _():
            up(halos, member, src).start()

        @pl.when(jnp.logical_and(has_prev, member <= n - 2))
        def _():
            down(halos, member, src).start()

    def k_copy(src, dst):
        return remote(k_src.at[dst], k_own.at[src], k_ss.at[dst], k_rs.at[src], device(plane, dst))

    def q_copy(src, dst):
        return remote(q_src.at[dst], q_own.at[src], q_ss.at[dst], q_rs.at[src], device(plane, dst))

    def v_copy(src, dst):
        return remote(v_src.at[dst], v_own.at[src], v_ss.at[dst], v_rs.at[src], device(plane, dst))

    forward(k_halos, me, k_src.at[me])
    for copy in (k_copy, q_copy, v_copy):
        for i in range(1, n):
            copy(me, to_peer(i)).start()
    forward(v_halos, me, v_src.at[me])
    keeps = [pltpu.make_async_copy(src.at[me], dst.at[me], loc_s.at[i])
             for i, (src, dst) in enumerate(((k_src, k_own), (q_src, q_own), (v_src, v_own)))]
    for keep in keeps:
        keep.start()

    def natural(src, dst):
        for h in range(heads):
            dst[h] = src[h * HDIM:(h + 1) * HDIM].T

    keeps[0].wait()
    natural(k_own.at[me], kn_own.at[me])

    def take_k(i, carry):
        source = from_peer(i)
        k_copy(source, me).wait_recv()
        forward(k_halos, source, k_own.at[source])
        natural(k_own.at[source], kn_own.at[source])
        return carry

    lax.fori_loop(1, n, take_k, 0)
    for keep in keeps[1:]:
        keep.wait()
    for i in range(1, n):
        q_copy(from_peer(i), me).wait_recv()

    factor = math.log2(math.e) / math.sqrt(HDIM)
    blocks = img.shape[0]
    lane = lax.broadcasted_iota(jnp.int32, (1, 2 * BLK), 1)
    base = plane * n
    pairs = n // 2

    def live_row(first, key_block):
        inside = jnp.logical_and(key_block >= 0, key_block < blocks)
        key_id = img[jnp.clip(key_block, 0, blocks - 1)]
        key_id = jnp.where(inside, key_id, -2)
        ids = jnp.where(lane < BLK, img[first], img[first + 1])
        return ids == key_id

    def weights(h, pair, keys, live, start, p_dst):
        q_pair = jnp.concatenate([q_own[2 * pair, pl.ds(h * HDIM, HDIM)],
                                  q_own[2 * pair + 1, pl.ds(h * HDIM, HDIM)]], axis=1)
        top = start
        for t in range(n):
            s = jnp.dot(keys(t), q_pair, preferred_element_type=jnp.float32)
            s_scr[h, t] = s
            top = jnp.maximum(top, jnp.where(live[t], jnp.max(s, axis=0, keepdims=True), NEG))
        total = jnp.zeros((8, 2 * BLK), jnp.float32)
        for t in range(n):
            shift = jnp.where(live[t], -top * factor, NEG)
            w = jnp.exp2(s_scr[h, t] * factor + shift)
            total = total + jnp.sum(w.reshape(BLK // 8, 8, 2 * BLK), axis=0)
            p_dst[t * BLK:(t + 1) * BLK] = w.astype(jnp.bfloat16)
        return top, jnp.sum(total, axis=0, keepdims=True)

    def times(values, p_src):
        v = jnp.concatenate([values(t) for t in range(n)], axis=1)
        return jnp.dot(v, p_src[...], preferred_element_type=jnp.float32)

    def take_v(i):
        source = from_peer(i)
        v_copy(source, me).wait_recv()
        forward(v_halos, source, v_own.at[source])

    def near(pair, carry):
        first = base + 2 * pair
        live = [live_row(first, base + t) for t in range(n)]
        for h in range(heads):
            at = pair * heads + h
            m_scr[at], l_scr[at] = weights(h, pair, lambda t: kn_own[t, h], live,
                                           jnp.full((1, 2 * BLK), NEG, jnp.float32), p_near.at[at])
        take_v(2 * pair + 1)

        @pl.when(pair < pairs - 1)
        def _():
            take_v(2 * pair + 2)
        return carry

    lax.fori_loop(0, pairs, near, 0)

    def take_halo(halos, src):
        @pl.when(has_prev)
        def _():
            for member in range(1, n):
                up(halos, member, src.at[member]).wait_recv()

        @pl.when(has_next)
        def _():
            for member in range(n - 1):
                down(halos, member, src.at[member]).wait_recv()

    take_halo(k_halos, k_own)

    def turn_halo(slot, carry):
        natural(k_halo.at[slot], kn_halo.at[slot])
        return carry

    lax.fori_loop(1, 2 * n - 1, turn_halo, 0)

    def far(pair, carry):
        first = base + 2 * pair
        live = []
        for t in range(n):
            slot = 2 * pair + 1 + t
            live.append(live_row(first, jnp.where(slot < n, base - n + slot, base + slot)))
        for h in range(heads):
            at = pair * heads + h
            top1 = m_scr[at]
            top, total = weights(h, pair, lambda t: kn_halo[2 * pair + 1 + t, h], live, top1, p_far.at[at])
            fade = jnp.exp2((top1 - top) * factor)
            out_t = times(lambda t: v_own[t, h * HDIM:(h + 1) * HDIM], p_near.at[at])
            acc[at] = out_t * fade
            l_scr[at] = l_scr[at] * fade + total
        return carry

    lax.fori_loop(0, pairs, far, 0)
    take_halo(v_halos, v_own)

    def out_copy(src, dst):
        return remote(o_src.at[dst], o_own.at[src], o_ss.at[dst], o_rs.at[src], device(plane, dst))

    def finish(step, carry):
        pair = (me // 2 + 1 + step) % pairs
        for h in range(heads):
            at = pair * heads + h
            out_t = times(lambda t: v_halo[2 * pair + 1 + t, h * HDIM:(h + 1) * HDIM], p_far.at[at])
            res = ((acc[at] + out_t) / l_scr[at]).astype(jnp.bfloat16)
            o_src[2 * pair, h * HDIM:(h + 1) * HDIM] = res[:, :BLK]
            o_src[2 * pair + 1, h * HDIM:(h + 1) * HDIM] = res[:, BLK:]
        for r in range(2):
            dst = 2 * pair + r

            @pl.when(dst != me)
            def _():
                out_copy(me, dst).start()

            @pl.when(dst == me)
            def _():
                pltpu.make_async_copy(o_src.at[me], o_own.at[me], loc_s.at[0]).start()
        return carry

    lax.fori_loop(0, pairs, finish, 0)

    pltpu.make_async_copy(o_src.at[me], o_own.at[me], loc_s.at[0]).wait()
    for i in range(1, n):
        out_copy(from_peer(i), me).wait_recv()
    flat = jnp.concatenate([o_own[member] for member in range(n)], axis=0)
    for c in range(0, n * cols, BLK):
        out[:, c:c + BLK] = flat[c:c + BLK].T

    for copy in (k_copy, q_copy, v_copy, out_copy):
        for i in range(1, n):
            copy(me, to_peer(i)).wait_send()

    for halos, src in ((k_halos, k_own), (v_halos, v_own)):
        @pl.when(has_next)
        def _():
            for member in range(1, n):
                up(halos, member, src.at[member]).wait_send()

        @pl.when(has_prev)
        def _():
            for member in range(n - 1):
                down(halos, member, src.at[member]).wait_send()


def solution(mesh):
    wide, grp = mesh.shape["wide"], mesh.shape["grp"]
    fold = MOST // grp
    n = fold * grp
    planes = wide // fold

    def body(query_rows, key_rows, value_rows, block_image):
        rows, width = query_rows.shape
        heads = width // HDIM // n
        cols = heads * HDIM
        bf, f32 = jnp.bfloat16, jnp.float32
        vmem = pl.BlockSpec(memory_space=pltpu.VMEM)
        hbm = pl.BlockSpec(memory_space=pl.ANY)
        dma = pltpu.SemaphoreType.DMA
        units = n // 2 * heads
        slices = pltpu.VMEM((n, cols, BLK), bf)
        return pl.pallas_call(
            functools.partial(kernel, (planes, fold, grp, heads)),
            out_shape=jax.ShapeDtypeStruct((rows, width), bf),
            in_specs=[pl.BlockSpec(memory_space=pltpu.SMEM), hbm, hbm, hbm],
            out_specs=vmem,
            scratch_shapes=[pltpu.VMEM((rows, width), bf)] * 3 + [slices] * 6 + [
                pltpu.VMEM((2 * n, cols, BLK), bf),
                pltpu.VMEM((2 * n, cols, BLK), bf),
                pltpu.VMEM((n, heads, BLK, HDIM), bf),
                pltpu.VMEM((2 * n, heads, BLK, HDIM), bf),
                pltpu.VMEM((units, 1, 2 * BLK), f32),
                pltpu.VMEM((units, 1, 2 * BLK), f32),
                pltpu.VMEM((units, HDIM, 2 * BLK), f32),
                pltpu.VMEM((heads, n, BLK, 2 * BLK), f32),
                pltpu.VMEM((units, n * BLK, 2 * BLK), bf),
                pltpu.VMEM((units, n * BLK, 2 * BLK), bf),
                slices, slices,
            ] + [dma((n,))] * 6 + [dma((n,)), dma((n,)), dma((2 * n,))] * 2 + [dma((n,)), dma((n,)), dma((3,))],
            compiler_params=pltpu.CompilerParams(collective_id=0, has_side_effects=True),
        )(block_image, query_rows, key_rows, value_rows)

    return jax.shard_map(
        body,
        mesh=mesh,
        in_specs=(
            P(("wide", "grp"), None),
            P(("wide", "grp"), None),
            P(("wide", "grp"), None),
            P(),
        ),
        out_specs=P(("wide", "grp"), None),
        check_vma=False,
    )
```

time: 34.2 us -> 32.8 us (0.959)
  Pallas kernels: 32.3 us -> 30.9 us
    pallas_call x1, Pallas kernels: 32.3 us -> 30.9 us  [body(): pl.pallas_call(functools.partial(kernel, (planes, fold, grp, heads)), out...]
where the time goes in v2:
time: 32.8 us; the launch traced here: 32.6 us
  Pallas kernels  30.9 us (94%)
  local copies, waits for them, and re-layouts  1.72 us (5%)
    pallas_call x1, Pallas kernels, body(): pl.pallas_call(functools.partial(kernel, (planes, fold, grp, heads)), out...  30.9 us
    unnamed x1, local copies, waits for them, and re-layouts  1.72 us

profile of v2, /device:TPU:1, one launch (start us, length us, event | category | flops | bytes accessed | tf_op | source)
XLA Modules:
  0.0 32.6 jit_solution(9937845748105914345)
XLA Ops:
  0.0 30.9 %shard_map.46 = bf16[128,1280]{1,0:T(8,128)(2,1)} custom-call(s32[32]{0:T(128)} %img.1, bf16[128,1280]{1,0:T(8,128)(2,1)} %q_hbm.1, bf16[128,1280]{1,0:T(8,128)(2,1)} %k_hbm.1, bf16[128,1280]{1,0:T(8,128)(2,1)} %v_hbm.1), custom_call_target="tpu_custom_call" | custom-call | tf_op jit(solution)/shard_map/pallas_call | solution.py:295
  30.9 1.7 %copy.6 = bf16[128,1280]{1,0:T(8,128)(2,1)} copy(bf16[128,1280]{1,0:T(8,128)(2,1)} %shard_map.46) | data formatting | bytes 655360

commit v3 on v2

--- a/solution.py
+++ b/solution.py
@@ -12,6 +12,7 @@
 BLK = 128
 MOST = 8
 NEG = -1e30
+EARLY = 4
 MESH = pl.DeviceIdType.MESH
 
 
@@ -35,10 +36,15 @@
     def device(at_plane, member):
         return (at_plane * fold + member // grp, member % grp)
 
-    def to_peer(i):
+    def turn_of(j):
+        return j % 2 * (n // 2 + j // 2) + (1 - j % 2) * (j // 2)
+
+    def to_peer(j):
+        i = turn_of(j)
         return ((fold_at + i // grp) % fold) * grp + (grp_at + i % grp) % grp
 
-    def from_peer(i):
+    def from_peer(j):
+        i = turn_of(j)
         return ((fold_at + fold - i // grp) % fold) * grp + (grp_at + grp - i % grp) % grp
 
     barrier = pltpu.get_barrier_semaphore()
@@ -107,9 +113,16 @@
         return remote(v_src.at[dst], v_own.at[src], v_ss.at[dst], v_rs.at[src], device(plane, dst))
 
     forward(k_halos, me, k_src.at[me])
-    for copy in (k_copy, q_copy, v_copy):
-        for i in range(1, n):
-            copy(me, to_peer(i)).start()
+    for i in range(1, n):
+        k_copy(me, to_peer(i)).start()
+    for i in range(1, EARLY + 1):
+        v_copy(me, to_peer(i)).start()
+    q_copy(me, me // 2 * 2 + 1 - me % 2).start()
+    for step in range(1, n // 2):
+        for r in range(2):
+            q_copy(me, (me // 2 + n // 2 - step) % (n // 2) * 2 + r).start()
+    for i in range(EARLY + 1, n):
+        v_copy(me, to_peer(i)).start()
     forward(v_halos, me, v_src.at[me])
     keeps = [pltpu.make_async_copy(src.at[me], dst.at[me], loc_s.at[i])
              for i, (src, dst) in enumerate(((k_src, k_own), (q_src, q_own), (v_src, v_own)))]
@@ -133,9 +146,13 @@
     lax.fori_loop(1, n, take_k, 0)
     for keep in keeps[1:]:
         keep.wait()
-    for i in range(1, n):
-        q_copy(from_peer(i), me).wait_recv()
-
+    def take_v(i):
+        source = from_peer(i)
+        v_copy(source, me).wait_recv()
+        forward(v_halos, source, v_own.at[source])
+
+    for i in range(1, EARLY + 1):
+        take_v(i)
     factor = math.log2(math.e) / math.sqrt(HDIM)
     blocks = img.shape[0]
     lane = lax.broadcasted_iota(jnp.int32, (1, 2 * BLK), 1)
@@ -169,23 +186,18 @@
         v = jnp.concatenate([values(t) for t in range(n)], axis=1)
         return jnp.dot(v, p_src[...], preferred_element_type=jnp.float32)
 
-    def take_v(i):
-        source = from_peer(i)
-        v_copy(source, me).wait_recv()
-        forward(v_halos, source, v_own.at[source])
-
-    def near(pair, carry):
+    def near(step, carry):
+        pair = (me // 2 + step) % pairs
+        for r in range(2):
+            @pl.when(2 * pair + r != me)
+            def _():
+                q_copy(2 * pair + r, me).wait_recv()
         first = base + 2 * pair
         live = [live_row(first, base + t) for t in range(n)]
         for h in range(heads):
             at = pair * heads + h
             m_scr[at], l_scr[at] = weights(h, pair, lambda t: kn_own[t, h], live,
                                            jnp.full((1, 2 * BLK), NEG, jnp.float32), p_near.at[at])
-        take_v(2 * pair + 1)
-
-        @pl.when(pair < pairs - 1)
-        def _():
-            take_v(2 * pair + 2)
         return carry
 
     lax.fori_loop(0, pairs, near, 0)
@@ -207,7 +219,10 @@
         natural(k_halo.at[slot], kn_halo.at[slot])
         return carry
 
-    lax.fori_loop(1, 2 * n - 1, turn_halo, 0)
+    cuts = [1 + (2 * n - 2) * i // (n - 1 - EARLY) for i in range(n - EARLY)]
+    for i in range(EARLY + 1, n):
+        take_v(i)
+        lax.fori_loop(cuts[i - EARLY - 1], cuts[i - EARLY], turn_halo, 0)
 
     def far(pair, carry):
         first = base + 2 * pair

time: 32.8 us -> 31.1 us (0.948)
  Pallas kernels: 30.9 us -> 29.2 us
    pallas_call x1, Pallas kernels: 30.9 us -> 29.2 us  [body(): pl.pallas_call(functools.partial(kernel, (planes, fold, grp, heads)), out...]
where the time goes in v3:
time: 31.1 us; the launch traced here: 31 us
  Pallas kernels  29.2 us (94%)
  local copies, waits for them, and re-layouts  1.72 us (6%)
    pallas_call x1, Pallas kernels, body(): pl.pallas_call(functools.partial(kernel, (planes, fold, grp, heads)), out...  29.2 us
    unnamed x1, local copies, waits for them, and re-layouts  1.72 us

profile of v3, /device:TPU:1, one launch (start us, length us, event | category | flops | bytes accessed | tf_op | source)
XLA Modules:
  0.0 31.0 jit_solution(7882767889536057410)
XLA Ops:
  0.0 29.2 %shard_map.46 = bf16[128,1280]{1,0:T(8,128)(2,1)} custom-call(s32[32]{0:T(128)} %img.1, bf16[128,1280]{1,0:T(8,128)(2,1)} %q_hbm.1, bf16[128,1280]{1,0:T(8,128)(2,1)} %k_hbm.1, bf16[128,1280]{1,0:T(8,128)(2,1)} %v_hbm.1), custom_call_target="tpu_custom_call" | custom-call | tf_op jit(solution)/shard_map/pallas_call | solution.py:310
  29.3 1.7 %copy.6 = bf16[128,1280]{1,0:T(8,128)(2,1)} copy(bf16[128,1280]{1,0:T(8,128)(2,1)} %shard_map.46) | data formatting | bytes 655360
